TPU v7x, 32 devices: a whole 2x2x4 slice. The times are simulated.
32 devices in a mesh: mp: 2 (over core), gx: 2 (over y), gy: 8 (over z, x).
Axes of the slice: x: 2, y: 2, z: 4, core: 2. Of those that a mesh axis runs over, the one named last changes fastest.
Arguments:
- action: bfloat16 [8, 24, 64, 1024], P(None, None, ('mp', 'gx'), 'gy'), may hold values from 0.049804688 to 2
- land_mask: int32 [64, 1024], P(('mp', 'gx'), 'gy'), may hold values 0 or 1
- bathymetry: float32 [64, 1024], P(('mp', 'gx', 'gy')), may hold values from 8 to 40
- surge: float32 [64, 1024], P(('mp', 'gx', 'gy')), may hold values from -3 to 3
- ocean_fields: float32 [4, 16, 64, 1024], P(None, None, ('mp', 'gx', 'gy')), may hold values from -2.5 to 2.5
- layer_share: float32 [16], replicated, may hold values from 0.5 to 2
Outputs:
- new_action: bfloat16 [8, 24, 64, 1024], P(None, None, ('mp', 'gx'), 'gy')
- new_fields: float32 [4, 16, 64, 1024], P(None, None, ('mp', 'gx', 'gy'))
All inputs are finite; a program needn't handle non-finite values. No bound on the sum of `land_mask` on one device may be relied on, other than what follows from the above.
Results may differ from a plain program's by a relative error of at most 0.0046.
Values may be sent and summed in bfloat16 or wider, within the bound.
A program may use at most 64 MiB of HBM per device.

v0:
```python
import math

import jax
import jax.numpy as jnp
from jax import lax
from jax.sharding import PartitionSpec as P

STEPS = 4


GRAVITY = 9.81
STEP_TIME = 14.0
CELL_SIZE = 500.0
FIRST_FREQ = 0.05
FREQ_RATIO = 1.1
MIXING = 0.2
PUSH_SCALE = 20.0
OUTSIDE_DEPTH = 20.0


def with_halo(cells, sides, width):
    for axis, dim in sides:
        count = lax.axis_size(axis)
        ends = count - 1
        head = lax.slice_in_dim(cells, 0, width, axis=dim)
        tail = lax.slice_in_dim(cells, cells.shape[dim] - width, cells.shape[dim], axis=dim)
        cells = jnp.concatenate(
            [
                lax.ppermute(tail, axis, [(i, (i + 1) % count) for i in range(ends)]),
                cells,
                lax.ppermute(head, axis, [((i + 1) % count, i) for i in range(ends)]),
            ],
            axis=dim,
        )
    return cells


def spectral_tables(band_count, direction_count):
    radian = (
        2.0
        * math.pi
        * FIRST_FREQ
        * jnp.power(FREQ_RATIO, jnp.arange(band_count).astype(jnp.float32))
    )
    angles = jnp.arange(direction_count).astype(jnp.float32) * (2.0 * math.pi / direction_count)
    return (radian, jnp.cos(angles), jnp.sin(angles))


def wave_coefficients(radian_freq, water_depth):
    angular = radian_freq[:, None, None]
    deep_number = angular * angular / GRAVITY
    wave_number = deep_number / jnp.sqrt(jnp.tanh(deep_number * water_depth[None]))
    twice_kh = 2.0 * wave_number * water_depth[None]
    shoal_ratio = 0.5 * (1.0 + twice_kh / jnp.sinh(twice_kh))
    group_speed = shoal_ratio * angular / wave_number
    bend_factor = angular / jnp.sinh(twice_kh)
    return (shoal_ratio, group_speed, bend_factor)


def velocities(
    group_speed,
    bend_factor,
    cosine_table,
    sine_table,
    mean_east,
    mean_north,
    slope_east,
    slope_north,
):
    cos_dir = cosine_table[None, :, None, None]
    sin_dir = sine_table[None, :, None, None]
    courant = STEP_TIME / CELL_SIZE
    turn_scale = STEP_TIME / (2.0 * CELL_SIZE * (2.0 * math.pi / cosine_table.shape[0]))
    step_east = courant * (group_speed[:, None] * cos_dir + mean_east[None, None])
    step_north = courant * (group_speed[:, None] * sin_dir + mean_north[None, None])
    raw_turn = (
        turn_scale
        * bend_factor[:, None]
        * (sin_dir * slope_east[None, None] - cos_dir * slope_north[None, None])
    )
    return (step_east, step_north, raw_turn / (1.0 + jnp.abs(raw_turn)))


def advance(padded, step_east, step_north, turn_rate, wet_cells):
    center = padded[:, :, 1:-1, 1:-1].astype(jnp.float32)
    west_side = padded[:, :, 1:-1, :-2].astype(jnp.float32)
    east_side = padded[:, :, 1:-1, 2:].astype(jnp.float32)
    south_side = padded[:, :, :-2, 1:-1].astype(jnp.float32)
    north_side = padded[:, :, 2:, 1:-1].astype(jnp.float32)
    advected = (
        center
        - jnp.maximum(step_east, 0.0) * (center - west_side)
        - jnp.minimum(step_east, 0.0) * (east_side - center)
        - jnp.maximum(step_north, 0.0) * (center - south_side)
        - jnp.minimum(step_north, 0.0) * (north_side - center)
    )
    before = jnp.roll(advected, 1, axis=1)
    following = jnp.roll(advected, -1, axis=1)
    turned = (
        advected
        - jnp.maximum(turn_rate, 0.0) * (advected - before)
        - jnp.minimum(turn_rate, 0.0) * (following - advected)
    )
    return (wet_cells[None, None] * turned).astype(jnp.bfloat16)


def stresses(spectrum, radian_freq, shoal_ratio, cosine_table, sine_table):
    energy = radian_freq[:, None, None, None] * spectrum.astype(jnp.float32)
    ratio = shoal_ratio[:, None]
    cos_sq = (cosine_table * cosine_table)[None, :, None, None]
    sin_sq = (sine_table * sine_table)[None, :, None, None]
    cross = (cosine_table * sine_table)[None, :, None, None]
    stress_xx = jnp.sum(energy * (ratio * (cos_sq + 1.0) - 0.5), axis=(0, 1))
    stress_xy = jnp.sum(energy * ratio * cross, axis=(0, 1))
    stress_yy = jnp.sum(energy * (ratio * (sin_sq + 1.0) - 0.5), axis=(0, 1))
    return jnp.stack([stress_xx, stress_xy, stress_yy])


def divergence(padded_stress, water_depth):
    east_diff = padded_stress[:, 1:-1, 2:] - padded_stress[:, 1:-1, :-2]
    north_diff = padded_stress[:, 2:, 1:-1] - padded_stress[:, :-2, 1:-1]
    force_east = -(east_diff[0] + north_diff[1]) / (2.0 * water_depth)
    force_north = -(east_diff[1] + north_diff[2]) / (2.0 * water_depth)
    return jnp.stack([force_east, force_north])


def vertical_mix(fields):
    upper = jnp.concatenate([fields[:, :1], fields[:, :-1]], axis=1)
    lower = jnp.concatenate([fields[:, 1:], fields[:, -1:]], axis=1)
    return fields + MIXING * (upper - 2.0 * fields + lower)


def apply_push(fields, forces, layer_weight):
    mixed = vertical_mix(fields)
    spare = jnp.zeros((fields.shape[0] - 2,) + forces.shape[1:], jnp.float32)
    forcing = jnp.concatenate([forces, spare], axis=0)
    return (
        mixed + PUSH_SCALE * fields.shape[1] * layer_weight[None, :, None, None] * forcing[:, None]
    )


def grid_mask(first_row, first_col, height, width, total_rows, total_cols, margin, inner):
    row_ids = first_row - margin + jnp.arange(height, dtype=jnp.int32)
    col_ids = first_col - margin + jnp.arange(width, dtype=jnp.int32)
    if inner:
        row_valid = (row_ids > 0) & (row_ids < total_rows - 1)
        col_valid = (col_ids > 0) & (col_ids < total_cols - 1)
    else:
        row_valid = (row_ids >= 0) & (row_ids < total_rows)
        col_valid = (col_ids >= 0) & (col_ids < total_cols)
    return (row_valid[:, None] & col_valid[None, :]).astype(jnp.float32)


def march_deep(
    spectrum,
    stacked,
    rim_width,
    coupled_halo,
    action_halo,
    first_row,
    first_col,
    total_rows,
    total_cols,
    radian_freq,
    cosine_table,
    sine_table,
):
    tile_rows = spectrum.shape[2]
    tile_cols = spectrum.shape[3]
    wide = coupled_halo(stacked)
    span_rows = tile_rows + 2 * rim_width - 2
    span_cols = tile_cols + 2 * rim_width - 2
    inside = grid_mask(
        first_row, first_col, span_rows, span_cols, total_rows, total_cols, rim_width - 1, False
    )
    near_depth = jnp.where(inside > 0.0, wide[2, 1:-1, 1:-1], OUTSIDE_DEPTH)
    slope_east = wide[2, 1:-1, 2:] - wide[2, 1:-1, :-2]
    slope_north = wide[2, 2:, 1:-1] - wide[2, :-2, 1:-1]
    wide_shoal, group_speed, bend_factor = wave_coefficients(radian_freq, near_depth)
    wide_east, wide_north, wide_turn = velocities(
        group_speed,
        bend_factor,
        cosine_table,
        sine_table,
        wide[0, 1:-1, 1:-1],
        wide[1, 1:-1, 1:-1],
        slope_east,
        slope_north,
    )
    wide_wet = wide[3, 1:-1, 1:-1]
    for group_index in range(STEPS // rim_width):
        current = action_halo(spectrum)
        for inner_step in range(rim_width):
            high_rows = span_rows - inner_step
            high_cols = span_cols - inner_step
            current = advance(
                current,
                wide_east[:, :, inner_step:high_rows, inner_step:high_cols],
                wide_north[:, :, inner_step:high_rows, inner_step:high_cols],
                wide_turn[:, :, inner_step:high_rows, inner_step:high_cols],
                wide_wet[inner_step:high_rows, inner_step:high_cols],
            )
        spectrum = current
    shoal_ratio = wide_shoal[
        :, rim_width - 1 : rim_width - 1 + tile_rows, rim_width - 1 : rim_width - 1 + tile_cols
    ]
    return (spectrum, shoal_ratio)


def shards(action, land_mask, bathymetry, surge, ocean_fields, layer_share):
    tile_rows = action.shape[2]
    tile_cols = action.shape[3]
    total_rows = tile_rows * lax.axis_size(("mp", "gx"))
    total_cols = tile_cols * lax.axis_size("gy")
    first_row = lax.axis_index(("mp", "gx")) * tile_rows
    first_col = lax.axis_index("gy") * tile_cols
    strip_depth = bathymetry + surge
    layer_weight = layer_share / jnp.sum(layer_share)
    mean_east = jnp.sum(layer_weight[:, None, None] * ocean_fields[0], axis=0)
    mean_north = jnp.sum(layer_weight[:, None, None] * ocean_fields[1], axis=0)
    coupled = lax.all_to_all(
        jnp.stack([mean_east, mean_north, strip_depth]),
        "gy",
        split_axis=2,
        concat_axis=1,
        tiled=True,
    )
    tile_east = coupled[0]
    tile_north = coupled[1]
    water_depth = coupled[2]
    wet_cells = land_mask.astype(jnp.float32) * grid_mask(
        first_row, first_col, tile_rows, tile_cols, total_rows, total_cols, 0, True
    )
    radian_freq, cosine_table, sine_table = spectral_tables(action.shape[0], action.shape[1])
    spectrum = action
    stacked = jnp.stack([tile_east, tile_north, water_depth, wet_cells])
    spectrum, shoal_ratio = march_deep(
        spectrum,
        stacked,
        2,
        lambda value: with_halo(value, ((("mp", "gx"), 1), ("gy", 2)), 2),
        lambda value: with_halo(value, ((("mp", "gx"), 2), ("gy", 3)), 2),
        first_row,
        first_col,
        total_rows,
        total_cols,
        radian_freq,
        cosine_table,
        sine_table,
    )
    stress_tile = stresses(spectrum, radian_freq, shoal_ratio, cosine_table, sine_table) / (
        action.shape[0] * action.shape[1]
    )
    padded_stress = with_halo(stress_tile, ((("mp", "gx"), 1), ("gy", 2)), 1)
    forces = lax.all_to_all(
        divergence(padded_stress, water_depth), "gy", split_axis=1, concat_axis=2, tiled=True
    )
    new_fields = apply_push(ocean_fields, forces, layer_weight)
    return (spectrum, new_fields)


def solution(mesh):
    return jax.shard_map(
        shards,
        mesh=mesh,
        in_specs=(
            P(None, None, ("mp", "gx"), "gy"),
            P(("mp", "gx"), "gy"),
            P(("mp", "gx", "gy"), None),
            P(("mp", "gx", "gy"), None),
            P(None, None, ("mp", "gx", "gy"), None),
            P(),
        ),
        out_specs=(P(None, None, ("mp", "gx"), "gy"), P(None, None, ("mp", "gx", "gy"), None)),
        check_vma=False,
    )
```

profile of v0, /device:TPU:0, one launch (start us, length us, event | category | flops | bytes accessed | tf_op | source)
XLA Modules:
  0.0 172.1 jit_solution(18235991453795992440)
XLA Ops:
  8.2 7.3 %all-to-all-start = ((f32[8,1,768]{2,1,0:T(1,128)}), f32[8,1,768]{2,1,0:T(1,128)S(1)}, u32[]{:S(2)}, u32[]{:S(2)}) async-start(f32[8,1,768]{2,1,0:T(1,128)} %reshape.200), calls=%async_computation | async-start | bytes 49152 | tf_op jit(solution)/shard_map/all_to_all | solution.py:221
  15.5 5.0 %copy.68 = bf16[8,24,16,128]{1,0,3,2:T(8,128)(2,1)} copy(bf16[8,24,16,128]{3,2,1,0:T(8,128)(2,1)} %param.6) | data formatting | bytes 1572864 | tf_op args[0]
  24.0 5.3 %collective-permute-start.4 = (bf16[8,24,2,128]{1,0,3,2:T(8,128)(2,1)}, bf16[8,24,2,128]{1,0,3,2:T(8,128)(2,1)}, u32[]{:S(2)}, u32[]{:S(2)}) collective-permute-start(bf16[8,24,2,128]{1,0,3,2:T(8,128)(2,1)} %get-tuple-element.20), channel_id=1, source_target_pairs={{0,8},{8,16},{16,24},{1,9},{9,17},{17,25},{2,10},{10,18},{18,26},{... | collective-permute-start | bytes 294920 | tf_op jit(solution)/shard_map/ppermute | solution.py:29
  32.9 3.2 %fusion.86 = (f32[1,8,2,128]{0,2,3,1:T(2,128)S(1)}, f32[1,8,2,128]{0,2,3,1:T(2,128)}, f32[1,8,2,128]{0,2,3,1:T(2,128)S(1)}) fusion(f32[3,8,2,128]{0,2,3,1:T(2,128)S(1)} %bitcast.44), kind=kLoop, calls=%fused_computation.206 | loop fusion | bytes 49152 | tf_op jit(solution)/shard_map/slice | solution.py:228
  39.8 4.5 %collective-permute-start = (f32[4,2,128]{2,0,1:T(4,128)S(1)}, f32[4,2,128]{2,0,1:T(4,128)S(1)}, u32[]{:S(2)}, u32[]{:S(2)}) collective-permute-start(f32[4,2,128]{2,0,1:T(4,128)S(1)} %get-tuple-element.68), channel_id=1, source_target_pairs={{0,8},{8,16},{16,24},{1,9},{9,17},{17,25},{2,10},{10,18},{18,26},{... | collective-permute-start | bytes 12296 | tf_op jit(solution)/shard_map/ppermute | solution.py:29
  47.1 4.6 %collective-permute-start.2 = (f32[4,20,2]{2,0,1:T(4,128)S(1)}, f32[4,20,2]{2,0,1:T(4,128)S(1)}, u32[]{:S(2)}, u32[]{:S(2)}) collective-permute-start(f32[4,20,2]{2,0,1:T(4,128)S(1)} %get-tuple-element.62), channel_id=1, source_target_pairs={{0,1},{1,2},{2,3},{3,4},{4,5},{5,6},{6,7},{8,9},{9,10},{10,11},{11... | collective-permute-start | bytes 1928 | tf_op jit(solution)/shard_map/ppermute | solution.py:29
  55.4 3.9 %pad_maximum_fusion = bf16[8,24,20,128]{1,0,3,2:T(8,128)(2,1)S(1)} fusion(bf16[8,24,2,128]{1,0,3,2:T(8,128)(2,1)} %collective-permute-done.5, bf16[8,24,16,128]{1,0,3,2:T(8,128)(2,1)} %copy.68, bf16[8,24,2,128]{1,0,3,2:T(8,128)(2,1)} %collective-permute-done.4), kind=kLoop, calls=%fused_computation.10 | loop fusion | flops 983040 | bytes 1966080 | tf_op jit(solution)/shard_map/concatenate | solution.py:27
  59.3 2.3 %copy-done = bf16[8,24,20,128]{1,0,3,2:T(8,128)(2,1)} copy-done((bf16[8,24,20,128]{1,0,3,2:T(8,128)(2,1)}, bf16[8,24,20,128]{1,0,3,2:T(8,128)(2,1)S(1)}, u32[]{:S(2)}) %copy-start) | copy-done | bytes 983064
  62.9 6.1 %collective-permute-start.6 = (bf16[8,24,20,2]{1,0,3,2:T(8,128)(2,1)S(1)}, bf16[8,24,20,2]{1,0,3,2:T(8,128)(2,1)}, u32[]{:S(2)}, u32[]{:S(2)}) collective-permute-start(bf16[8,24,20,2]{1,0,3,2:T(8,128)(2,1)S(1)} %get-tuple-element.18), channel_id=1, source_target_pairs={{0,1},{1,2},{2,3},{3,4},{4,5},{5,6},{6,7},{8,9},{9,10},{10,11},{11... | collective-permute-start | bytes 46088 | tf_op jit(solution)/shard_map/ppermute | solution.py:29
  69.1 4.9 %copy.72 = bf16[8,24,20,128]{3,1,2,0:T(8,128)(2,1)S(1)} copy(bf16[8,24,20,128]{1,0,3,2:T(8,128)(2,1)} %copy-done) | data formatting | bytes 1966080 | tf_op jit(solution)/shard_map/concatenate | solution.py:27
  78.2 5.1 %fusion.4 = (f32[8,24,18,130]{3,1,2,0:T(8,128)S(1)}, f32[8,24,18,130]{3,1,2,0:T(8,128)S(1)}, f32[8,24,18,130]{3,1,2,0:T(8,128)S(1)}) fusion(bf16[8,24,20,132]{3,1,2,0:T(8,128)(2,1)S(1)} %pad_maximum_fusion.1, bf16[8,24,20,2]{3,1,2,0:T(8,128)(2,1)S(1)} %copy.73, bf16[8,24,20,128]{3,1,2,0:T(8,128)(2,1)S(1)} %copy.72, bf16[8,24,20,2]{3,1,2,0:T(8,128)(2,1)S(1)} %copy.71, ...), kind=kLoop, calls=%fused_computation.17 | loop fusion | flops 14826240 | bytes 9194592 | tf_op jit(solution)/shard_map/sub | solution.py:91
  84.7 2.9 %multiply_divide_fusion = (f32[8,24,18,130]{3,1,2,0:T(8,128)S(1)}, bf16[8,24,18,130]{3,1,2,0:T(8,128)(2,1)S(1)}) fusion(f32[24,18,130]{2,0,1:T(8,128)S(1)} %multiply_subtract_fusion, f32[8,18,130]{2,1,0:T(8,128)S(1)} %copy-done.5, f32[8,24,18,130]{3,1,2,0:T(8,128)S(1)} %get-tuple-element.51, f32[8,1,18,130]{3,1,2,0:T(1,128)S(1)} %get-tuple-element.28, ...), kind=kLoop, calls=%fused_computation.11 | loop fusion | flops 7188480 | bytes 8395920 | tf_op jit(solution)/shard_map/div | solution.py:81
  92.1 4.8 %collective-permute-start.8 = (bf16[8,24,2,128]{3,1,2,0:T(8,128)(2,1)S(1)}, bf16[8,24,2,128]{3,1,2,0:T(8,128)(2,1)S(1)}, u32[]{:S(2)}, u32[]{:S(2)}) collective-permute-start(bf16[8,24,2,128]{3,1,2,0:T(8,128)(2,1)S(1)} %get-tuple-element.43), channel_id=1, source_target_pairs={{0,8},{8,16},{16,24},{1,9},{9,17},{17,25},{2,10},{10,18},{18,26},{... | collective-permute-start | bytes 294920 | tf_op jit(solution)/shard_map/ppermute | solution.py:29
  104.9 6.0 %collective-permute-start.10 = (bf16[8,24,20,2]{1,0,3,2:T(8,128)(2,1)S(1)}, bf16[8,24,20,2]{1,0,3,2:T(8,128)(2,1)}, u32[]{:S(2)}, u32[]{:S(2)}) collective-permute-start(bf16[8,24,20,2]{1,0,3,2:T(8,128)(2,1)S(1)} %copy.92), channel_id=1, source_target_pairs={{0,1},{1,2},{2,3},{3,4},{4,5},{5,6},{6,7},{8,9},{9,10},{10,11},{11... | collective-permute-start | bytes 46088 | tf_op jit(solution)/shard_map/ppermute | solution.py:29
  117.7 6.1 %fusion.11 = f32[8,24,18,130]{3,1,2,0:T(8,128)S(1)} fusion(bf16[8,24,20,132]{3,1,2,0:T(8,128)(2,1)S(1)} %pad_maximum_fusion.2, bf16[8,24,20,2]{3,1,2,0:T(8,128)(2,1)S(1)} %copy.81, bf16[8,24,2,128]{3,1,2,0:T(8,128)(2,1)S(1)} %collective-permute-done.9, bf16[8,24,16,128]{3,1,2,0:T(8,128)(2,1)S(1)} %fusion.47, bf16[8,24,2,128]{3,1,2,0:T(8,128)(2,1)S(1)} %copy-done.9, ...), kind=kLoop, calls=%fused_computation.24 | loop fusion | flops 18420480 | bytes 5600352 | tf_op jit(solution)/shard_map/sub | solution.py:91
  124.7 2.9 %fusion.25 = bf16[8,24,18,130]{3,1,2,0:T(8,128)(2,1)S(1)} fusion(f32[8,24,18,130]{3,1,2,0:T(8,128)S(1)} %fusion.11, f32[8,23,18,130]{3,1,2,0:T(8,128)S(1)} %get-tuple-element.23, f32[8,1,18,130]{3,1,2,0:T(1,128)S(1)} %get-tuple-element.25, f32[8,1,18,130]{3,1,2,0:T(1,128)S(1)} %get-tuple-element.24, f32[8,23,18,130]{3,1,2,0:T(8,128)S(1)} %get-tuple-element.22, ...), kind=kLoop, calls=%fused_computation.41 | loop fusion | flops 7188480 | bytes 6598800 | tf_op jit(solution)/shard_map/convert_element_type | solution.py:104
  127.6 4.7 %fusion.39 = f32[8,24,16,128]{3,1,2,0:T(8,128)S(1)} fusion(f32[8,24,18,130]{3,1,2,0:T(8,128)} %copy-done.2, f32[8,24,18,130]{3,1,2,0:T(8,128)} %copy-done.3, bf16[8,24,18,130]{3,1,2,0:T(8,128)(2,1)S(1)} %fusion.25), kind=kLoop, calls=%fused_computation.78 | loop fusion | flops 8257536 | bytes 8650752 | tf_op jit(solution)/shard_map/sub | solution.py:91
  133.1 3.3 %multiply_reduce_fusion.2 = (f32[16,128]{1,0:T(8,128)S(1)}, f32[16,128]{1,0:T(8,128)S(1)}, f32[16,128]{1,0:T(8,128)S(1)}, bf16[8,24,16,128]{3,1,2,0:T(8,128)(2,1)S(1)}) fusion(f32[24]{0:T(128)S(1)} %copy-done.22, f32[8,16,128]{2,1,0:T(8,128)S(1)} %copy-done.10, f32[8]{0:T(128)S(1)} %copy-done.20, f32[24]{0:T(128)S(1)} %copy-done.23, f32[24]{0:T(128)S(1)} %copy-done.21, ...), kind=kLoop, calls=%fused_computation.100 | loop fusion | flops 9824256 | bytes 7176512 | tf_op jit(solution)/shard_map/reduce_sum | solution.py:113
  136.5 4.4 %collective-permute-start.12 = (f32[3,1,128]{2,0,1:T(4,128)S(1)}, f32[3,1,128]{2,0,1:T(4,128)S(1)}, u32[]{:S(2)}, u32[]{:S(2)}) collective-permute-start(f32[3,1,128]{2,0,1:T(4,128)S(1)} %get-tuple-element.67), channel_id=1, source_target_pairs={{0,8},{8,16},{16,24},{1,9},{9,17},{17,25},{2,10},{10,18},{18,26},{... | collective-permute-start | bytes 4616 | tf_op jit(solution)/shard_map/ppermute | solution.py:29
  142.2 4.2 %collective-permute-done.13 = f32[3,1,128]{2,0,1:T(4,128)S(1)} collective-permute-done((f32[3,1,128]{2,0,1:T(4,128)S(1)}, f32[3,1,128]{2,0,1:T(4,128)S(1)}, u32[]{:S(2)}, u32[]{:S(2)}) %collective-permute-start.13) | collective-permute-done | bytes 1568 | tf_op jit(solution)/shard_map/ppermute | solution.py:31
  146.4 4.2 %collective-permute-start.15 = (f32[3,18,1]{2,0,1:T(4,128)S(1)}, f32[3,18,1]{2,0,1:T(4,128)S(1)}, u32[]{:S(2)}, u32[]{:S(2)}) collective-permute-start(f32[3,18,1]{2,0,1:T(4,128)S(1)} %get-tuple-element.65), channel_id=1, source_target_pairs={{0,1},{1,2},{2,3},{3,4},{4,5},{5,6},{6,7},{8,9},{9,10},{10,11},{11... | collective-permute-start | bytes 656 | tf_op jit(solution)/shard_map/ppermute | solution.py:29
  152.3 4.9 %collective-permute-done.14 = f32[3,18,1]{2,0,1:T(4,128)S(1)} collective-permute-done((f32[3,18,1]{2,0,1:T(4,128)S(1)}, f32[3,18,1]{2,0,1:T(4,128)S(1)}, u32[]{:S(2)}, u32[]{:S(2)}) %collective-permute-start.14) | collective-permute-done | bytes 248 | tf_op jit(solution)/shard_map/ppermute | solution.py:31
  158.1 6.0 %all-to-all-start.1 = ((f32[2,16,128]{2,0,1:T(2,128)}), f32[2,16,128]{2,0,1:T(2,128)S(1)}, u32[]{:S(2)}, u32[]{:S(2)}) async-start(f32[2,16,128]{2,0,1:T(2,128)} %pad_maximum_fusion.28), calls=%async_computation.1 | async-start | bytes 32768 | tf_op jit(solution)/shard_map/all_to_all | solution.py:255
  165.1 5.6 %all-to-all-done.1 = f32[2,16,128]{2,0,1:T(2,128)S(1)} async-done(((f32[2,16,128]{2,0,1:T(2,128)}), f32[2,16,128]{2,0,1:T(2,128)S(1)}, u32[]{:S(2)}, u32[]{:S(2)}) %all-to-all-start.1) | async-done | bytes 16416 | tf_op jit(solution)/shard_map/all_to_all | solution.py:255
  (144 shorter events, 58.6 us)
Async XLA Ops:
  8.2 22.0 %all-to-all-start = ((f32[8,1,768]{2,1,0:T(1,128)}), f32[8,1,768]{2,1,0:T(1,128)S(1)}, u32[]{:S(2)}, u32[]{:S(2)}) async-start(f32[8,1,768]{2,1,0:T(1,128)} %reshape.200), calls=%async_computation | async-start | bytes 49152 | tf_op jit(solution)/shard_map/all_to_all | solution.py:221
  15.5 14.6 %copy-start.13 = (s32[16,128]{1,0:T(8,128)S(1)}, s32[16,128]{1,0:T(8,128)}, u32[]{:S(2)}) copy-start(s32[16,128]{1,0:T(8,128)} %param.7) | copy-start | bytes 24580
  22.7 32.7 %collective-permute-start.5 = (bf16[8,24,2,128]{1,0,3,2:T(8,128)(2,1)}, bf16[8,24,2,128]{1,0,3,2:T(8,128)(2,1)}, u32[]{:S(2)}, u32[]{:S(2)}) collective-permute-start(bf16[8,24,2,128]{1,0,3,2:T(8,128)(2,1)} %get-tuple-element.21), channel_id=1, source_target_pairs={{8,0},{16,8},{24,16},{9,1},{17,9},{25,17},{10,2},{18,10},{26,18},{... | collective-permute-start | bytes 294920 | tf_op jit(solution)/shard_map/ppermute | solution.py:31
  24.0 31.4 %collective-permute-start.4 = (bf16[8,24,2,128]{1,0,3,2:T(8,128)(2,1)}, bf16[8,24,2,128]{1,0,3,2:T(8,128)(2,1)}, u32[]{:S(2)}, u32[]{:S(2)}) collective-permute-start(bf16[8,24,2,128]{1,0,3,2:T(8,128)(2,1)} %get-tuple-element.20), channel_id=1, source_target_pairs={{0,8},{8,16},{16,24},{1,9},{9,17},{17,25},{2,10},{10,18},{18,26},{... | collective-permute-start | bytes 294920 | tf_op jit(solution)/shard_map/ppermute | solution.py:29
  30.0 48.2 %copy-start.14 = (f32[24]{0:T(128)}, f32[24]{0:T(128)S(1)}, u32[]{:S(2)}) copy-start(f32[24]{0:T(128)S(1)} %get-tuple-element.76) | copy-start | bytes 292
  30.0 48.2 %copy-start.16 = (f32[24]{0:T(128)}, f32[24]{0:T(128)S(1)}, u32[]{:S(2)}) copy-start(f32[24]{0:T(128)S(1)} %get-tuple-element.77) | copy-start | bytes 292
  30.2 23.9 %copy-start.19 = (f32[8]{0:T(128)}, f32[8]{0:T(128)S(1)}, u32[]{:S(2)}) copy-start(f32[8]{0:T(128)S(1)} %fusion.73) | copy-start | bytes 100
  38.5 5.9 %collective-permute-start.1 = (f32[4,2,128]{2,0,1:T(4,128)S(1)}, f32[4,2,128]{2,0,1:T(4,128)S(1)}, u32[]{:S(2)}, u32[]{:S(2)}) collective-permute-start(f32[4,2,128]{2,0,1:T(4,128)S(1)} %get-tuple-element.69), channel_id=1, source_target_pairs={{8,0},{16,8},{24,16},{9,1},{17,9},{25,17},{10,2},{18,10},{26,18},{... | collective-permute-start | bytes 12296 | tf_op jit(solution)/shard_map/ppermute | solution.py:31
  39.8 5.9 %collective-permute-start = (f32[4,2,128]{2,0,1:T(4,128)S(1)}, f32[4,2,128]{2,0,1:T(4,128)S(1)}, u32[]{:S(2)}, u32[]{:S(2)}) collective-permute-start(f32[4,2,128]{2,0,1:T(4,128)S(1)} %get-tuple-element.68), channel_id=1, source_target_pairs={{0,8},{8,16},{16,24},{1,9},{9,17},{17,25},{2,10},{10,18},{18,26},{... | collective-permute-start | bytes 12296 | tf_op jit(solution)/shard_map/ppermute | solution.py:29
  45.8 5.9 %collective-permute-start.3 = (f32[4,20,2]{2,0,1:T(4,128)S(1)}, f32[4,20,2]{2,0,1:T(4,128)S(1)}, u32[]{:S(2)}, u32[]{:S(2)}) collective-permute-start(f32[4,20,2]{2,0,1:T(4,128)S(1)} %get-tuple-element.63), channel_id=1, source_target_pairs={{1,0},{2,1},{3,2},{4,3},{5,4},{6,5},{7,6},{9,8},{10,9},{11,10},{12... | collective-permute-start | bytes 1928 | tf_op jit(solution)/shard_map/ppermute | solution.py:31
  47.1 6.2 %collective-permute-start.2 = (f32[4,20,2]{2,0,1:T(4,128)S(1)}, f32[4,20,2]{2,0,1:T(4,128)S(1)}, u32[]{:S(2)}, u32[]{:S(2)}) collective-permute-start(f32[4,20,2]{2,0,1:T(4,128)S(1)} %get-tuple-element.62), channel_id=1, source_target_pairs={{0,1},{1,2},{2,3},{3,4},{4,5},{5,6},{6,7},{8,9},{9,10},{10,11},{11... | collective-permute-start | bytes 1928 | tf_op jit(solution)/shard_map/ppermute | solution.py:29
  61.6 12.4 %collective-permute-start.7 = (bf16[8,24,20,2]{1,0,3,2:T(8,128)(2,1)S(1)}, bf16[8,24,20,2]{1,0,3,2:T(8,128)(2,1)S(1)}, u32[]{:S(2)}, u32[]{:S(2)}) collective-permute-start(bf16[8,24,20,2]{1,0,3,2:T(8,128)(2,1)S(1)} %get-tuple-element.19), channel_id=1, source_target_pairs={{1,0},{2,1},{3,2},{4,3},{5,4},{6,5},{7,6},{9,8},{10,9},{11,10},{12... | collective-permute-start | bytes 46088 | tf_op jit(solution)/shard_map/ppermute | solution.py:31
  62.9 12.1 %collective-permute-start.6 = (bf16[8,24,20,2]{1,0,3,2:T(8,128)(2,1)S(1)}, bf16[8,24,20,2]{1,0,3,2:T(8,128)(2,1)}, u32[]{:S(2)}, u32[]{:S(2)}) collective-permute-start(bf16[8,24,20,2]{1,0,3,2:T(8,128)(2,1)S(1)} %get-tuple-element.18), channel_id=1, source_target_pairs={{0,1},{1,2},{2,3},{3,4},{4,5},{5,6},{6,7},{8,9},{9,10},{10,11},{11... | collective-permute-start | bytes 46088 | tf_op jit(solution)/shard_map/ppermute | solution.py:29
  90.8 6.8 %collective-permute-start.9 = (bf16[8,24,2,128]{3,1,2,0:T(8,128)(2,1)S(1)}, bf16[8,24,2,128]{3,1,2,0:T(8,128)(2,1)S(1)}, u32[]{:S(2)}, u32[]{:S(2)}) collective-permute-start(bf16[8,24,2,128]{3,1,2,0:T(8,128)(2,1)S(1)} %get-tuple-element.44), channel_id=1, source_target_pairs={{8,0},{16,8},{24,16},{9,1},{17,9},{25,17},{10,2},{18,10},{26,18},{... | collective-permute-start | bytes 294920 | tf_op jit(solution)/shard_map/ppermute | solution.py:31
  92.1 7.4 %collective-permute-start.8 = (bf16[8,24,2,128]{3,1,2,0:T(8,128)(2,1)S(1)}, bf16[8,24,2,128]{3,1,2,0:T(8,128)(2,1)S(1)}, u32[]{:S(2)}, u32[]{:S(2)}) collective-permute-start(bf16[8,24,2,128]{3,1,2,0:T(8,128)(2,1)S(1)} %get-tuple-element.43), channel_id=1, source_target_pairs={{0,8},{8,16},{16,24},{1,9},{9,17},{17,25},{2,10},{10,18},{18,26},{... | collective-permute-start | bytes 294920 | tf_op jit(solution)/shard_map/ppermute | solution.py:29
  102.4 10.1 %collective-permute-start.11 = (bf16[8,24,20,2]{1,0,3,2:T(8,128)(2,1)}, bf16[8,24,20,2]{1,0,3,2:T(8,128)(2,1)S(1)}, u32[]{:S(2)}, u32[]{:S(2)}) collective-permute-start(bf16[8,24,20,2]{1,0,3,2:T(8,128)(2,1)} %copy.93), channel_id=1, source_target_pairs={{1,0},{2,1},{3,2},{4,3},{5,4},{6,5},{7,6},{9,8},{10,9},{11,10},{12... | collective-permute-start | bytes 46088 | tf_op jit(solution)/shard_map/ppermute | solution.py:31
  104.9 8.7 %collective-permute-start.10 = (bf16[8,24,20,2]{1,0,3,2:T(8,128)(2,1)S(1)}, bf16[8,24,20,2]{1,0,3,2:T(8,128)(2,1)}, u32[]{:S(2)}, u32[]{:S(2)}) collective-permute-start(bf16[8,24,20,2]{1,0,3,2:T(8,128)(2,1)S(1)} %copy.92), channel_id=1, source_target_pairs={{0,1},{1,2},{2,3},{3,4},{4,5},{5,6},{6,7},{8,9},{9,10},{10,11},{11... | collective-permute-start | bytes 46088 | tf_op jit(solution)/shard_map/ppermute | solution.py:29
  133.1 18.8 %copy-start.4 = (f32[4,16,2,1024]{3,2,1,0:T(2,128)S(1)}, f32[4,16,2,1024]{3,2,1,0:T(2,128)}, u32[]{:S(2)}) copy-start(f32[4,16,2,1024]{3,2,1,0:T(2,128)} %param.10) | copy-start | bytes 1572868
  136.4 34.3 %copy-start.18 = (f32[16]{0:T(128)S(1)}, f32[16]{0:T(128)}, u32[]{:S(2)}) copy-start(f32[16]{0:T(128)} %get-tuple-element.15) | copy-start | bytes 196
  136.5 5.7 %collective-permute-start.12 = (f32[3,1,128]{2,0,1:T(4,128)S(1)}, f32[3,1,128]{2,0,1:T(4,128)S(1)}, u32[]{:S(2)}, u32[]{:S(2)}) collective-permute-start(f32[3,1,128]{2,0,1:T(4,128)S(1)} %get-tuple-element.67), channel_id=1, source_target_pairs={{0,8},{8,16},{16,24},{1,9},{9,17},{17,25},{2,10},{10,18},{18,26},{... | collective-permute-start | bytes 4616 | tf_op jit(solution)/shard_map/ppermute | solution.py:29
  140.9 5.5 %collective-permute-start.13 = (f32[3,1,128]{2,0,1:T(4,128)S(1)}, f32[3,1,128]{2,0,1:T(4,128)S(1)}, u32[]{:S(2)}, u32[]{:S(2)}) collective-permute-start(f32[3,1,128]{2,0,1:T(4,128)S(1)} %get-tuple-element.66), channel_id=1, source_target_pairs={{8,0},{16,8},{24,16},{9,1},{17,9},{25,17},{10,2},{18,10},{26,18},{... | collective-permute-start | bytes 4616 | tf_op jit(solution)/shard_map/ppermute | solution.py:31
  146.4 5.8 %collective-permute-start.15 = (f32[3,18,1]{2,0,1:T(4,128)S(1)}, f32[3,18,1]{2,0,1:T(4,128)S(1)}, u32[]{:S(2)}, u32[]{:S(2)}) collective-permute-start(f32[3,18,1]{2,0,1:T(4,128)S(1)} %get-tuple-element.65), channel_id=1, source_target_pairs={{0,1},{1,2},{2,3},{3,4},{4,5},{5,6},{6,7},{8,9},{9,10},{10,11},{11... | collective-permute-start | bytes 656 | tf_op jit(solution)/shard_map/ppermute | solution.py:29
  150.6 6.6 %collective-permute-start.14 = (f32[3,18,1]{2,0,1:T(4,128)S(1)}, f32[3,18,1]{2,0,1:T(4,128)S(1)}, u32[]{:S(2)}, u32[]{:S(2)}) collective-permute-start(f32[3,18,1]{2,0,1:T(4,128)S(1)} %get-tuple-element.64), channel_id=1, source_target_pairs={{1,0},{2,1},{3,2},{4,3},{5,4},{6,5},{7,6},{9,8},{10,9},{11,10},{12... | collective-permute-start | bytes 656 | tf_op jit(solution)/shard_map/ppermute | solution.py:31
  158.1 12.6 %all-to-all-start.1 = ((f32[2,16,128]{2,0,1:T(2,128)}), f32[2,16,128]{2,0,1:T(2,128)S(1)}, u32[]{:S(2)}, u32[]{:S(2)}) async-start(f32[2,16,128]{2,0,1:T(2,128)} %pad_maximum_fusion.28), calls=%async_computation.1 | async-start | bytes 32768 | tf_op jit(solution)/shard_map/all_to_all | solution.py:255
  (18 other events, 40.0 us)
where the time goes:
time: 173 us; the launch traced here: 172 us
  starting transfers between devices  63.7 us (37%)
  other arithmetic  47.9 us (28%)
  local copies, waits for them, and re-layouts  39.5 us (23%)
  waiting for transfers between devices  19.6 us (11%)
    ppermute x8, starting transfers between devices, with_halo(): lax.ppermute(tail, axis, [(i, (i + 1) % count) for i in range(ends)])  39.9 us
    sub x4, other arithmetic, advance(): center - jnp.maximum(step_east, 0.0) * (center - west_side)  17.6 us
    unnamed x57, local copies, waits for them, and re-layouts  16.1 us
    ppermute x8, starting transfers between devices, with_halo(): lax.ppermute(head, axis, [((i + 1) % count, i) for i in range(ends)])  10.5 us
    ppermute x8, waiting for transfers between devices, with_halo(): lax.ppermute(head, axis, [((i + 1) % count, i) for i in range(ends)])  9.19 us
    concatenate x7, other arithmetic, with_halo(): jnp.concatenate([lax.ppermute(tail, axis, [(i, (i + 1) % count) for i in...  7.51 us
    all_to_all x1, starting transfers between devices, shards(): lax.all_to_all(jnp.stack([mean_east, mean_north, strip_depth]), 'gy', spl...  7.25 us
    all_to_all x1, starting transfers between devices, shards(): lax.all_to_all(divergence(padded_stress, water_depth), 'gy', split_axis=1...  5.99 us
  transfers between devices with their start and end apart: 18, of which 7 were waited for; matrix products, arithmetic and copies ran while one was open for 17% of the time, Pallas kernels for 0%

commit v1 on v0

v1 whole, which is shorter than its diff:
```python
import functools
import math

import jax
import jax.numpy as jnp
import numpy as np
from jax import lax
from jax.experimental import pallas as pl
from jax.experimental.pallas import tpu as pltpu
from jax.sharding import PartitionSpec as P

STEPS = 4
GRAVITY = 9.81
STEP_TIME = 14.0
CELL_SIZE = 500.0
FIRST_FREQ = 0.05
FREQ_RATIO = 1.1
MIXING = 0.2
PUSH_SCALE = 20.0
LANES = 128
TOP = 8
MESH = pl.DeviceIdType.MESH


def kernel(
    mesh_mp,
    mesh_gx,
    n,
    action_ref,
    land_ref,
    bath_ref,
    surge_ref,
    ocean_ref,
    share_ref,
    out_ref,
    fields_ref,
    pk,
    rx,
    tile,
    dpad,
    dhalo,
    ccg,
    sn,
    hs,
    tb,
    qs,
    xs,
    ps,
    ew_send,
    ew_recv,
    ns_send,
    ns_recv,
    st,
    spad,
    shalo,
    pk2,
    rx2,
    a2a_send,
    a2a_recv,
    back_send,
    back_recv,
    dep_send,
    dep_recv,
    str_send,
    str_recv,
    ew_ssem,
    ew_rsem,
    ns_ssem,
    ns_rsem,
):
    freqs, dirs, rows, cols = action_ref.shape
    levels, strip = ocean_ref.shape[1], ocean_ref.shape[2]
    wide = ocean_ref.shape[3]
    row_count = mesh_mp * mesh_gx
    mp, gx, me = lax.axis_index("mp"), lax.axis_index("gx"), lax.axis_index("gy")
    rank = mp * mesh_gx + gx
    has_south, has_north = rank > 0, rank < row_count - 1
    has_west, has_east = me > 0, me < n - 1
    south_rank = lax.rem(rank + row_count - 1, row_count)
    north_rank = lax.rem(rank + 1, row_count)
    south = (lax.div(south_rank, mesh_gx), lax.rem(south_rank, mesh_gx), me)
    north = (lax.div(north_rank, mesh_gx), lax.rem(north_rank, mesh_gx), me)
    west = (mp, gx, lax.rem(me + n - 1, n))
    east = (mp, gx, lax.rem(me + 1, n))
    angles = np.arange(dirs) * (2.0 * math.pi / dirs)
    cosine = [float(np.float32(v)) for v in np.cos(angles)]
    sine = [float(np.float32(v)) for v in np.sin(angles)]
    courant = STEP_TIME / CELL_SIZE
    turn_scale = STEP_TIME / (2.0 * CELL_SIZE * (2.0 * math.pi / dirs))

    barrier = pltpu.get_barrier_semaphore()
    for off in range(1, n):
        pl.semaphore_signal(
            barrier, inc=1, device_id=(mp, gx, lax.rem(me + off, n)), device_id_type=MESH
        )

    @pl.when(has_south)
    def _():
        pl.semaphore_signal(barrier, inc=1, device_id=south, device_id_type=MESH)

    @pl.when(has_north)
    def _():
        pl.semaphore_signal(barrier, inc=1, device_id=north, device_id_type=MESH)

    total = share_ref[0]
    for level in range(1, levels):
        total = total + share_ref[level]
    total_row = jnp.full((strip, wide), total, jnp.float32)
    for field in range(2):
        mean = share_ref[0] * ocean_ref[field, 0]
        for level in range(1, levels):
            mean = mean + share_ref[level] * ocean_ref[field, level]
        pk[field * strip : (field + 1) * strip, :] = mean / total_row
    pk[2 * strip : 3 * strip, :] = bath_ref[...] + surge_ref[...]
    wide_lane = lax.broadcasted_iota(jnp.int32, (8, wide), 1)

    def east_diff(value):
        after = jnp.where(wide_lane == wide - 1, 0.0, pltpu.roll(value, wide - 1, 1))
        before = jnp.where(wide_lane == 0, 0.0, pltpu.roll(value, 1, 1))
        return after - before

    pk[8:16, :] = east_diff(pk[0:8, :])
    pk[3 * strip : 4 * strip, :] = pk[8 + 2 * strip : 8 + 3 * strip, :]

    pl.semaphore_wait(barrier, n - 1 + has_south.astype(jnp.int32) + has_north.astype(jnp.int32))

    def strip_copy(off):
        peer = lax.rem(me + off, n)
        return pltpu.make_async_remote_copy(
            src_ref=pk.at[0:8, pl.ds(pl.multiple_of(peer * LANES, LANES), LANES)],
            dst_ref=rx.at[me],
            send_sem=a2a_send.at[off],
            recv_sem=a2a_recv.at[off],
            device_id=(mp, gx, peer),
            device_id_type=MESH,
        )

    for off in range(1, n):
        strip_copy(off).start()
    rx[me] = pk[0:8, pl.ds(pl.multiple_of(me * LANES, LANES), LANES)]

    def ew_copy(step, freq, side):
        return pltpu.make_async_remote_copy(
            src_ref=ew_send.at[step, freq],
            dst_ref=ew_recv.at[side, step, freq],
            send_sem=ew_ssem.at[side, step, freq],
            recv_sem=ew_rsem.at[side, step, freq],
            device_id=east if side == 0 else west,
            device_id_type=MESH,
        )

    def ns_copy(step, freq, side):
        return pltpu.make_async_remote_copy(
            src_ref=ns_send.at[side, step, freq],
            dst_ref=ns_recv.at[side, step, freq],
            send_sem=ns_ssem.at[side, step, freq],
            recv_sem=ns_rsem.at[side, step, freq],
            device_id=north if side == 0 else south,
            device_id_type=MESH,
        )

    def send_edges(step, freq):
        @pl.when(has_east)
        def _():
            ew_copy(step, freq, 0).start()

        @pl.when(has_west)
        def _():
            ew_copy(step, freq, 1).start()

        @pl.when(has_north)
        def _():
            ns_copy(step, freq, 0).start()

        @pl.when(has_south)
        def _():
            ns_copy(step, freq, 1).start()

    def recv_edges(step, freq):
        @pl.when(has_west)
        def _():
            ew_copy(step, freq, 0).wait_recv()

        @pl.when(has_east)
        def _():
            ew_copy(step, freq, 1).wait_recv()

        @pl.when(has_south)
        def _():
            ns_copy(step, freq, 0).wait_recv()

        @pl.when(has_north)
        def _():
            ns_copy(step, freq, 1).wait_recv()

    def drain_edges(step, freq):
        @pl.when(has_east)
        def _():
            ew_copy(step, freq, 0).wait_send()

        @pl.when(has_west)
        def _():
            ew_copy(step, freq, 1).wait_send()

        @pl.when(has_north)
        def _():
            ns_copy(step, freq, 0).wait_send()

        @pl.when(has_south)
        def _():
            ns_copy(step, freq, 1).wait_send()

    @pl.when(jnp.logical_not(has_west))
    def _():
        ew_recv[0] = jnp.zeros(ew_recv.shape[1:], jnp.float32)

    @pl.when(jnp.logical_not(has_east))
    def _():
        ew_recv[1] = jnp.zeros(ew_recv.shape[1:], jnp.float32)

    @pl.when(jnp.logical_not(has_south))
    def _():
        ns_recv[0] = jnp.zeros(ns_recv.shape[1:], jnp.float32)
        dhalo[0] = jnp.zeros(dhalo.shape[1:], jnp.float32)
        shalo[0] = jnp.zeros(shalo.shape[1:], jnp.float32)

    @pl.when(jnp.logical_not(has_north))
    def _():
        ns_recv[1] = jnp.zeros(ns_recv.shape[1:], jnp.float32)
        dhalo[1] = jnp.zeros(dhalo.shape[1:], jnp.float32)
        shalo[1] = jnp.zeros(shalo.shape[1:], jnp.float32)

    lane = lax.broadcasted_iota(jnp.int32, (rows, cols), 1)
    pair = lane // 2
    even = lane % 2 == 0
    first_lane, last_lane = lane == 0, lane == cols - 1

    def keep(step, freq, d, value, packed):
        xs[freq, d, TOP : TOP + rows, :] = value
        ns_send[0, step, freq, d : d + 1, :] = value[rows - 1 : rows, :]
        ns_send[1, step, freq, d : d + 1, :] = value[0:1, :]
        turned = pltpu.roll(value, 2 * d + 1, 1)
        return jnp.where(pair == d, turned, packed)

    def first_edges(freq, carry):
        packed = jnp.zeros((rows, cols), jnp.float32)
        for d in range(dirs):
            packed = keep(0, freq, d, action_ref[freq, d].astype(jnp.float32), packed)
        ew_send[0, freq] = packed
        send_edges(0, freq)
        return carry

    lax.fori_loop(0, freqs, first_edges, 0)

    for field in range(ocean_ref.shape[0]):
        for level in range(levels):
            here = ocean_ref[field, level]
            upper = ocean_ref[field, max(level - 1, 0)]
            lower = ocean_ref[field, min(level + 1, levels - 1)]
            fields_ref[field, level] = here + MIXING * (upper - 2.0 * here + lower)

    for off in range(1, n):
        strip_copy(off).wait_recv()
    for g in range(n):
        for item in range(4):
            tile[item, g * strip : (g + 1) * strip, :] = rx[g, item * strip : (item + 1) * strip, :]

    def depth_copy(side):
        return pltpu.make_async_remote_copy(
            src_ref=tile.at[2, rows - 8 : rows] if side == 0 else tile.at[2, 0:8],
            dst_ref=dhalo.at[side],
            send_sem=dep_send.at[side],
            recv_sem=dep_recv.at[side],
            device_id=north if side == 0 else south,
            device_id_type=MESH,
        )

    def stress_copy(side):
        return pltpu.make_async_remote_copy(
            src_ref=st.at[1:3, rows - 8 : rows] if side == 0 else st.at[1:3, 0:8],
            dst_ref=shalo.at[side],
            send_sem=str_send.at[side],
            recv_sem=str_recv.at[side],
            device_id=north if side == 0 else south,
            device_id_type=MESH,
        )

    def start_pair(copy):
        @pl.when(has_north)
        def _():
            copy(0).start()

        @pl.when(has_south)
        def _():
            copy(1).start()

    def wait_pair(copy):
        @pl.when(has_south)
        def _():
            copy(0).wait_recv()

        @pl.when(has_north)
        def _():
            copy(1).wait_recv()

    def drain_pair(copy):
        @pl.when(has_north)
        def _():
            copy(0).wait_send()

        @pl.when(has_south)
        def _():
            copy(1).wait_send()

    start_pair(depth_copy)
    depth = tile[2]
    share_of = 1.0 / (freqs * dirs)
    for f in range(freqs):
        sigma = 2.0 * math.pi * FIRST_FREQ * FREQ_RATIO**f
        deep = sigma * sigma / GRAVITY
        number = deep / jnp.sqrt(jnp.tanh(deep * depth))
        twice = 2.0 * number * depth
        grown = jnp.exp(twice)
        inv_sinh = 2.0 / (grown - 1.0 / grown)
        ratio = 0.5 * (1.0 + twice * inv_sinh)
        ccg[f] = (courant * sigma) * ratio / number
        tb[f] = (turn_scale * sigma) * inv_sinh
        sn[f] = (sigma * share_of) * ratio
        hs[f] = jnp.full((rows, cols), 0.5 * sigma * share_of, jnp.float32)
    dpad[TOP : TOP + rows, :] = depth
    wait_pair(depth_copy)
    dpad[TOP - 1 : TOP, :] = dhalo[0, 7:8, :]
    dpad[TOP + rows : TOP + rows + 1, :] = dhalo[1, 0:1, :]
    slope_north = dpad[TOP + 1 : TOP + 1 + rows, :] - dpad[TOP - 1 : TOP - 1 + rows, :]
    slope_east = tile[3]
    for d in range(dirs // 2):
        ps[d] = sine[d] * slope_east - cosine[d] * slope_north

    def turn_rates(freq, carry):
        scale = tb[freq]
        for d in range(dirs // 2):
            raw = scale * ps[d]
            qs[freq, d] = raw / (1.0 + jnp.abs(raw))
        return carry

    lax.fori_loop(0, freqs, turn_rates, 0)
    row = lax.broadcasted_iota(jnp.int32, (rows, cols), 0) + rank * rows
    col = lane + me * cols
    inner = (row > 0) & (row < row_count * rows - 1) & (col > 0) & (col < wide - 1)
    tile[3] = jnp.where(inner, land_ref[...].astype(jnp.float32), 0.0)
    tile[0] = courant * tile[0]
    tile[1] = courant * tile[1]

    def advance(index, carry):
        step, freq = lax.div(index, freqs), lax.rem(index, freqs)
        recv_edges(step, freq)
        merged = jnp.where(
            even,
            pltpu.roll(ew_recv[1, step, freq], cols - 1, 1),
            pltpu.roll(ew_recv[0, step, freq], 1, 1),
        )
        speed = ccg[freq]
        mean_east, mean_north = tile[0], tile[1]
        for d in range(dirs):
            xs[freq, d, TOP - 1 : TOP, :] = ns_recv[0, step, freq, d : d + 1, :]
            xs[freq, d, TOP + rows : TOP + rows + 1, :] = ns_recv[1, step, freq, d : d + 1, :]
        for d in range(dirs):
            value = xs[freq, d, TOP : TOP + rows, :]
            below = xs[freq, d, TOP - 1 : TOP - 1 + rows, :]
            above = xs[freq, d, TOP + 1 : TOP + 1 + rows, :]
            edge = pltpu.roll(merged, cols - 2 * d - 1, 1)
            left = jnp.where(first_lane, edge, pltpu.roll(value, 1, 1))
            right = jnp.where(last_lane, edge, pltpu.roll(value, cols - 1, 1))
            ax = speed * cosine[d] + mean_east
            ay = speed * sine[d] + mean_north
            ps[d] = (
                value
                - jnp.abs(ax) * (value - jnp.where(ax > 0.0, left, right))
                - jnp.abs(ay) * (value - jnp.where(ay > 0.0, below, above))
            )
        wet = tile[3]
        after = lax.rem(step + 1, STEPS)
        packed = jnp.zeros((rows, cols), jnp.float32)
        for d in range(dirs):
            half = d % (dirs // 2)
            rate = qs[freq, half]
            value = ps[d]
            before, following = ps[(d - 1) % dirs], ps[(d + 1) % dirs]
            if d >= dirs // 2:
                before, following = following, before
            turned = value - jnp.abs(rate) * (value - jnp.where(rate > 0.0, before, following))
            rounded = (wet * turned).astype(jnp.bfloat16)
            out_ref[freq, d] = rounded
            value = rounded.astype(jnp.float32)
            xs[freq, d, TOP : TOP + rows, :] = value
            packed = jnp.where(pair == d, pltpu.roll(value, 2 * d + 1, 1), packed)

        @pl.when(step < STEPS - 1)
        def _():
            ew_send[after, freq] = packed
            for d in range(dirs):
                ns_send[0, after, freq, d : d + 1, :] = xs[
                    freq, d, TOP + rows - 1 : TOP + rows, :
                ]
                ns_send[1, after, freq, d : d + 1, :] = xs[freq, d, TOP : TOP + 1, :]
            send_edges(after, freq)

        return carry

    lax.fori_loop(0, STEPS * freqs, advance, 0)

    def stress(freq, carry):
        plain = jnp.zeros((rows, cols), jnp.float32)
        cos_sq, cross = plain, plain
        for d in range(dirs):
            value = xs[freq, d, TOP : TOP + rows, :]
            plain = plain + value
            cos_sq = cos_sq + (cosine[d] * cosine[d]) * value
            cross = cross + (cosine[d] * sine[d]) * value
        scaled, half = sn[freq], hs[freq] * plain
        return (
            carry[0] + scaled * (cos_sq + plain) - half,
            carry[1] + scaled * cross,
            carry[2] + scaled * (2.0 * plain - cos_sq) - half,
        )

    zero = jnp.zeros((rows, cols), jnp.float32)
    sums = lax.fori_loop(0, freqs, stress, (zero, zero, zero))
    for item in range(3):
        st[item] = sums[item]
    start_pair(stress_copy)
    for item in range(2):
        spad[item, TOP : TOP + rows, :] = sums[1 + item]
    wait_pair(stress_copy)
    for item in range(2):
        spad[item, TOP - 1 : TOP, :] = shalo[0, item, 7:8, :]
        spad[item, TOP + rows : TOP + rows + 1, :] = shalo[1, item, 0:1, :]
    for item in range(2):
        tile[item] = (
            spad[item, TOP + 1 : TOP + 1 + rows, :] - spad[item, TOP - 1 : TOP - 1 + rows, :]
        )
    for g in range(n):
        span = slice(g * strip, (g + 1) * strip)
        pk2[g, 0:strip, :] = st[0, span, :]
        pk2[g, strip : 2 * strip, :] = st[1, span, :]
        pk2[g, 2 * strip : 3 * strip, :] = tile[0, span, :]
        pk2[g, 3 * strip : 4 * strip, :] = tile[1, span, :]
    mine = pl.ds(pl.multiple_of(me * LANES, LANES), LANES)

    def back_copy(off):
        peer = lax.rem(me + off, n)
        return pltpu.make_async_remote_copy(
            src_ref=pk2.at[peer],
            dst_ref=rx2.at[0:8, mine],
            send_sem=back_send.at[off],
            recv_sem=back_recv.at[off],
            device_id=(mp, gx, peer),
            device_id_type=MESH,
        )

    for off in range(1, n):
        back_copy(off).start()
    rx2[0:8, mine] = pk2[me]
    for off in range(1, n):
        back_copy(off).wait_recv()
    rx2[8:16, :] = east_diff(rx2[0:8, :])
    scale = (-0.5 * PUSH_SCALE * levels) / (pk[2 * strip : 3 * strip, :] * total_row)
    for field in range(2):
        force = scale * (
            rx2[8 + field * strip : 8 + (field + 1) * strip, :]
            + rx2[(2 + field) * strip : (3 + field) * strip, :]
        )
        for level in range(levels):
            fields_ref[field, level] = fields_ref[field, level] + share_ref[level] * force

    for off in range(1, n):
        strip_copy(off).wait_send()
        back_copy(off).wait_send()
    drain_pair(depth_copy)
    drain_pair(stress_copy)

    def drain(index, carry):
        drain_edges(lax.div(index, freqs), lax.rem(index, freqs))
        return carry

    lax.fori_loop(0, STEPS * freqs, drain, 0)


def shards(mesh, action, land_mask, bathymetry, surge, ocean_fields, layer_share):
    freqs, dirs, rows, cols = action.shape
    n = mesh.shape["gy"]
    wide = ocean_fields.shape[3]
    f32 = jnp.float32
    dma = pltpu.SemaphoreType.DMA
    vmem = pl.BlockSpec(memory_space=pltpu.VMEM)
    cells = (rows, cols)
    padded = rows + 2 * TOP
    return pl.pallas_call(
        functools.partial(kernel, mesh.shape["mp"], mesh.shape["gx"], n),
        out_shape=(
            jax.ShapeDtypeStruct(action.shape, action.dtype),
            jax.ShapeDtypeStruct(ocean_fields.shape, ocean_fields.dtype),
        ),
        in_specs=[vmem] * 5 + [pl.BlockSpec(memory_space=pltpu.SMEM)],
        out_specs=(vmem, vmem),
        scratch_shapes=[
            pltpu.VMEM((16, wide), f32),
            pltpu.VMEM((n, 8, cols), f32),
            pltpu.VMEM((4,) + cells, f32),
            pltpu.VMEM((padded, cols), f32),
            pltpu.VMEM((2, 8, cols), f32),
            pltpu.VMEM((freqs,) + cells, f32),
            pltpu.VMEM((freqs,) + cells, f32),
            pltpu.VMEM((freqs,) + cells, f32),
            pltpu.VMEM((freqs,) + cells, f32),
            pltpu.VMEM((freqs, dirs // 2) + cells, f32),
            pltpu.VMEM((freqs, dirs, padded, cols), f32),
            pltpu.VMEM((dirs,) + cells, f32),
            pltpu.VMEM((STEPS, freqs) + cells, f32),
            pltpu.VMEM((2, STEPS, freqs) + cells, f32),
            pltpu.VMEM((2, STEPS, freqs, dirs, cols), f32),
            pltpu.VMEM((2, STEPS, freqs, dirs, cols), f32),
            pltpu.VMEM((3,) + cells, f32),
            pltpu.VMEM((2, padded, cols), f32),
            pltpu.VMEM((2, 2, 8, cols), f32),
            pltpu.VMEM((n, 8, cols), f32),
            pltpu.VMEM((16, wide), f32),
            dma((n,)),
            dma((n,)),
            dma((n,)),
            dma((n,)),
            dma((2,)),
            dma((2,)),
            dma((2,)),
            dma((2,)),
            dma((2, STEPS, freqs)),
            dma((2, STEPS, freqs)),
            dma((2, STEPS, freqs)),
            dma((2, STEPS, freqs)),
        ],
        compiler_params=pltpu.CompilerParams(
            collective_id=0, has_side_effects=True, vmem_limit_bytes=40 * 1024 * 1024
        ),
    )(action, land_mask, bathymetry, surge, ocean_fields, layer_share)


def solution(mesh):
    return jax.shard_map(
        functools.partial(shards, mesh),
        mesh=mesh,
        in_specs=(
            P(None, None, ("mp", "gx"), "gy"),
            P(("mp", "gx"), "gy"),
            P(("mp", "gx", "gy"), None),
            P(("mp", "gx", "gy"), None),
            P(None, None, ("mp", "gx", "gy"), None),
            P(),
        ),
        out_specs=(P(None, None, ("mp", "gx"), "gy"), P(None, None, ("mp", "gx", "gy"), None)),
        check_vma=False,
    )
```

time: 173 us -> 44.9 us (0.26)
  starting transfers between devices: 63.7 us -> 0 us
  other arithmetic: 47.9 us -> 0 us
  Pallas kernels: 0 us -> 37.3 us
  local copies, waits for them, and re-layouts: 39.5 us -> 6.59 us
  waiting for transfers between devices: 19.6 us -> 0 us
    ppermute x16 -> x0, starting transfers between devices: 50.4 us -> none  [the longest x8 39.9 us: with_halo(): lax.ppermute(tail, axis, [(i, (i + 1) % count) for i in range(ends)])]
    pallas_call x0 -> x1, Pallas kernels: none -> 37.3 us  [shards(): pl.pallas_call(functools.partial(kernel, mesh.shape['mp'], mesh.shape['gx...]
    sub x7 -> x0, other arithmetic: 18.3 us -> none  [the longest x4 17.6 us: advance(): center - jnp.maximum(step_east, 0.0) * (center - west_side)]
    ppermute x16 -> x0, waiting for transfers between devices: 14 us -> none  [the longest x8 9.19 us: with_halo(): lax.ppermute(head, axis, [((i + 1) % count, i) for i in range(ends)])]
    all_to_all x2 -> x0, starting transfers between devices: 13.2 us -> none  [the longest x1 7.25 us: shards(): lax.all_to_all(jnp.stack([mean_east, mean_north, strip_depth]), 'gy', spl...]
    slice x22 -> x0, local copies, waits for them, and re-layouts: 11.4 us -> none  [the longest x2 3.68 us: shards(): tile_east = coupled[0]]
    unnamed x57 -> x14, local copies, waits for them, and re-layouts: 16.1 us -> 6.59 us
    concatenate x7 -> x0, other arithmetic: 7.51 us -> none  [with_halo(): jnp.concatenate([lax.ppermute(tail, axis, [(i, (i + 1) % count) for i in...]
  transfers between devices with their start and end apart: 18 -> 0, of which waited for: 7 -> 0; matrix products, arithmetic and copies ran while one was open for 17% -> 0% of each run, Pallas kernels for 0% -> 0%
where the time goes in v1:
time: 44.9 us; the launch traced here: 44.5 us
  Pallas kernels  37.3 us (83%)
  local copies, waits for them, and re-layouts  6.59 us (15%)
  between operations  0.65 us (1%)
    pallas_call x1, Pallas kernels, shards(): pl.pallas_call(functools.partial(kernel, mesh.shape['mp'], mesh.shape['gx...  37.3 us
    unnamed x14, local copies, waits for them, and re-layouts  6.59 us

profile of v1, /device:TPU:0, one launch (start us, length us, event | category | flops | bytes accessed | tf_op | source)
XLA Modules:
  0.0 44.5 jit_solution(8123476563323071830)
XLA Ops:
  0.6 0.0 copy-start
  0.6 1.1 %copy-done = bf16[8,24,16,128]{3,2,1,0:T(8,128)(2,1)S(1)} copy-done((bf16[8,24,16,128]{3,2,1,0:T(8,128)(2,1)S(1)}, bf16[8,24,16,128]{3,2,1,0:T(8,128)(2,1)}, u32[]{:S(2)}) %copy-start) | copy-done | bytes 786456
  1.8 0.0 copy-start.1
  1.8 1.0 %copy-done.1 = f32[4,16,2,1024]{3,2,1,0:T(2,128)S(1)} copy-done((f32[4,16,2,1024]{3,2,1,0:T(2,128)S(1)}, f32[4,16,2,1024]{3,2,1,0:T(2,128)}, u32[]{:S(2)}) %copy-start.1) | copy-done | bytes 524312
  2.8 0.0 copy-start.2
  2.8 0.7 %copy-done.2 = s32[16,128]{1,0:T(8,128)S(1)} copy-done((s32[16,128]{1,0:T(8,128)S(1)}, s32[16,128]{1,0:T(8,128)}, u32[]{:S(2)}) %copy-start.2) | copy-done | bytes 8216
  3.5 0.0 copy-start.3
  3.5 0.7 %copy-done.3 = f32[2,1024]{1,0:T(2,128)S(1)} copy-done((f32[2,1024]{1,0:T(2,128)S(1)}, f32[2,1024]{1,0:T(2,128)}, u32[]{:S(2)}) %copy-start.3) | copy-done | bytes 8216
  4.2 0.0 copy-start.4
  4.2 0.7 %copy-done.4 = f32[2,1024]{1,0:T(2,128)S(1)} copy-done((f32[2,1024]{1,0:T(2,128)S(1)}, f32[2,1024]{1,0:T(2,128)}, u32[]{:S(2)}) %copy-start.4) | copy-done | bytes 8216
  4.9 0.0 copy-start.5
  4.9 0.7 %copy-done.5 = f32[16]{0:T(128)S(1)} copy-done((f32[16]{0:T(128)S(1)}, f32[16]{0:T(128)}, u32[]{:S(2)}) %copy-start.5) | copy-done | bytes 88
  5.6 37.3 %shard_map.77 = (bf16[8,24,16,128]{3,2,1,0:T(8,128)(2,1)S(1)}, f32[4,16,2,1024]{3,2,1,0:T(2,128)S(1)}) custom-call(bf16[8,24,16,128]{3,2,1,0:T(8,128)(2,1)S(1)} %copy-done, s32[16,128]{1,0:T(8,128)S(1)} %copy-done.2, f32[2,1024]{1,0:T(2,128)S(1)} %copy-done.3, f32[2,1024]{1,0:T(2,128)S(1)} %copy-done.4, f32[4,16,2,1024]{3,2,1,0:T(2,128)S(1)} %copy-done.1, ...), custom_call_target="tpu_custom_call" | custom-call | tf_op jit(solution)/shard_map/pallas_call | solution.py:498
  42.9 0.9 %copy.10 = bf16[8,24,16,128]{3,2,1,0:T(8,128)(2,1)} copy(bf16[8,24,16,128]{3,2,1,0:T(8,128)(2,1)S(1)} %get-tuple-element.4) | data formatting | bytes 1572864
  43.7 0.8 %copy.11 = f32[4,16,2,1024]{3,2,1,0:T(2,128)} copy(f32[4,16,2,1024]{3,2,1,0:T(2,128)S(1)} %get-tuple-element.5) | data formatting | bytes 1048576
Async XLA Ops:
  0.6 1.1 %copy-start = (bf16[8,24,16,128]{3,2,1,0:T(8,128)(2,1)S(1)}, bf16[8,24,16,128]{3,2,1,0:T(8,128)(2,1)}, u32[]{:S(2)}) copy-start(bf16[8,24,16,128]{3,2,1,0:T(8,128)(2,1)} %action_ref.1) | copy-start | bytes 2359300
  1.8 1.0 %copy-start.1 = (f32[4,16,2,1024]{3,2,1,0:T(2,128)S(1)}, f32[4,16,2,1024]{3,2,1,0:T(2,128)}, u32[]{:S(2)}) copy-start(f32[4,16,2,1024]{3,2,1,0:T(2,128)} %ocean_ref.1) | copy-start | bytes 1572868
  2.8 0.7 %copy-start.2 = (s32[16,128]{1,0:T(8,128)S(1)}, s32[16,128]{1,0:T(8,128)}, u32[]{:S(2)}) copy-start(s32[16,128]{1,0:T(8,128)} %land_ref.1) | copy-start | bytes 24580
  3.5 0.7 %copy-start.3 = (f32[2,1024]{1,0:T(2,128)S(1)}, f32[2,1024]{1,0:T(2,128)}, u32[]{:S(2)}) copy-start(f32[2,1024]{1,0:T(2,128)} %bath_ref.1) | copy-start | bytes 24580
  4.2 0.7 %copy-start.4 = (f32[2,1024]{1,0:T(2,128)S(1)}, f32[2,1024]{1,0:T(2,128)}, u32[]{:S(2)}) copy-start(f32[2,1024]{1,0:T(2,128)} %surge_ref.1) | copy-start | bytes 24580
  4.9 0.7 %copy-start.5 = (f32[16]{0:T(128)S(1)}, f32[16]{0:T(128)}, u32[]{:S(2)}) copy-start(f32[16]{0:T(128)} %share_ref.1) | copy-start | bytes 196

commit v2 on v1

--- a/solution.py
+++ b/solution.py
@@ -26,15 +26,22 @@
     mesh_mp,
     mesh_gx,
     n,
+    action_in,
+    land_in,
+    bath_in,
+    surge_in,
+    ocean_in,
+    share_ref,
+    out_ref,
+    fields_ref,
     action_ref,
     land_ref,
     bath_ref,
     surge_ref,
     ocean_ref,
-    share_ref,
-    out_ref,
-    fields_ref,
+    in_sem,
     pk,
+    pk1,
     rx,
     tile,
     dpad,
@@ -88,6 +95,21 @@
     courant = STEP_TIME / CELL_SIZE
     turn_scale = STEP_TIME / (2.0 * CELL_SIZE * (2.0 * math.pi / dirs))
 
+    loads = [
+        pltpu.make_async_copy(source, target, in_sem.at[index])
+        for index, (source, target) in enumerate(
+            (
+                (ocean_in.at[0:2], ocean_ref.at[0:2]),
+                (bath_in, bath_ref),
+                (surge_in, surge_ref),
+                (action_in, action_ref),
+                (ocean_in.at[2:4], ocean_ref.at[2:4]),
+                (land_in, land_ref),
+            )
+        )
+    ]
+    for load in loads:
+        load.start()
     barrier = pltpu.get_barrier_semaphore()
     for off in range(1, n):
         pl.semaphore_signal(
@@ -102,6 +124,8 @@
     def _():
         pl.semaphore_signal(barrier, inc=1, device_id=north, device_id_type=MESH)
 
+    for load in loads[:3]:
+        load.wait()
     total = share_ref[0]
     for level in range(1, levels):
         total = total + share_ref[level]
@@ -122,12 +146,14 @@
     pk[8:16, :] = east_diff(pk[0:8, :])
     pk[3 * strip : 4 * strip, :] = pk[8 + 2 * strip : 8 + 3 * strip, :]
 
+    for g in range(n):
+        pk1[g] = pk[0:8, g * LANES : (g + 1) * LANES]
     pl.semaphore_wait(barrier, n - 1 + has_south.astype(jnp.int32) + has_north.astype(jnp.int32))
 
     def strip_copy(off):
         peer = lax.rem(me + off, n)
         return pltpu.make_async_remote_copy(
-            src_ref=pk.at[0:8, pl.ds(pl.multiple_of(peer * LANES, LANES), LANES)],
+            src_ref=pk1.at[peer],
             dst_ref=rx.at[me],
             send_sem=a2a_send.at[off],
             recv_sem=a2a_recv.at[off],
@@ -137,7 +163,7 @@
 
     for off in range(1, n):
         strip_copy(off).start()
-    rx[me] = pk[0:8, pl.ds(pl.multiple_of(me * LANES, LANES), LANES)]
+    rx[me] = pk1[me]
 
     def ew_copy(step, freq, side):
         return pltpu.make_async_remote_copy(
@@ -250,7 +276,10 @@
         send_edges(0, freq)
         return carry
 
+    loads[3].wait()
     lax.fori_loop(0, freqs, first_edges, 0)
+    loads[4].wait()
+    loads[5].wait()
 
     for field in range(ocean_ref.shape[0]):
         for level in range(levels):
@@ -501,10 +530,17 @@
             jax.ShapeDtypeStruct(action.shape, action.dtype),
             jax.ShapeDtypeStruct(ocean_fields.shape, ocean_fields.dtype),
         ),
-        in_specs=[vmem] * 5 + [pl.BlockSpec(memory_space=pltpu.SMEM)],
+        in_specs=[pl.BlockSpec(memory_space=pltpu.HBM)] * 5 + [pl.BlockSpec(memory_space=pltpu.SMEM)],
         out_specs=(vmem, vmem),
         scratch_shapes=[
+            pltpu.VMEM(action.shape, action.dtype),
+            pltpu.VMEM(land_mask.shape, land_mask.dtype),
+            pltpu.VMEM(bathymetry.shape, f32),
+            pltpu.VMEM(surge.shape, f32),
+            pltpu.VMEM(ocean_fields.shape, f32),
+            dma((6,)),
             pltpu.VMEM((16, wide), f32),
+            pltpu.VMEM((n, 8, cols), f32),
             pltpu.VMEM((n, 8, cols), f32),
             pltpu.VMEM((4,) + cells, f32),
             pltpu.VMEM((padded, cols), f32),
@@ -539,7 +575,7 @@
             dma((2, STEPS, freqs)),
         ],
         compiler_params=pltpu.CompilerParams(
-            collective_id=0, has_side_effects=True, vmem_limit_bytes=40 * 1024 * 1024
+            collective_id=0, has_side_effects=True, vmem_limit_bytes=60 * 1024 * 1024
         ),
     )(action, land_mask, bathymetry, surge, ocean_fields, layer_share)
 

time: 44.9 us -> 42.1 us (0.938)
  local copies, waits for them, and re-layouts: 6.59 us -> 3 us
  Pallas kernels: 37.3 us -> 38.3 us
    unnamed x14 -> x4, local copies, waits for them, and re-layouts: 6.59 us -> 3 us
    pallas_call x1, Pallas kernels: 37.3 us -> 38.3 us  [shards(): pl.pallas_call(functools.partial(kernel, mesh.shape['mp'], mesh.shape['gx...]
where the time goes in v2:
time: 42.1 us; the launch traced here: 41.9 us
  Pallas kernels  38.3 us (91%)
  local copies, waits for them, and re-layouts  3 us (7%)
  between operations  0.65 us (2%)
    pallas_call x1, Pallas kernels, shards(): pl.pallas_call(functools.partial(kernel, mesh.shape['mp'], mesh.shape['gx...  38.3 us
    unnamed x4, local copies, waits for them, and re-layouts  3 us

profile of v2, /device:TPU:0, one launch (start us, length us, event | category | flops | bytes accessed | tf_op | source)
XLA Modules:
  0.0 41.9 jit_solution(1952174246487919539)
XLA Ops:
  0.6 38.3 %shard_map.77 = (bf16[8,24,16,128]{3,2,1,0:T(8,128)(2,1)}, f32[4,16,2,1024]{3,2,1,0:T(2,128)}) custom-call(bf16[8,24,16,128]{3,2,1,0:T(8,128)(2,1)} %action_in.1, s32[16,128]{1,0:T(8,128)} %land_in.1, f32[2,1024]{1,0:T(2,128)} %bath_in.1, f32[2,1024]{1,0:T(2,128)} %surge_in.1, f32[4,16,2,1024]{3,2,1,0:T(2,128)} %ocean_in.1, f32[16]{0:T(128)} %share_ref.1), custom_call_target="tpu_custom_call" | custom-call | tf_op jit(solution)/shard_map/pallas_call | solution.py:527
  38.9 0.0 copy-start
  38.9 2.2 %copy.10 = bf16[8,24,16,128]{3,2,1,0:T(8,128)(2,1)} copy(bf16[8,24,16,128]{3,2,1,0:T(8,128)(2,1)} %get-tuple-element.4) | data formatting | bytes 1572864
  41.1 0.0 copy-done
  41.1 0.8 %copy.11 = f32[4,16,2,1024]{3,2,1,0:T(2,128)} copy(f32[4,16,2,1024]{3,2,1,0:T(2,128)S(1)} %copy-done) | data formatting | bytes 1048576
Async XLA Ops:
  38.9 2.2 %copy-start = (f32[4,16,2,1024]{3,2,1,0:T(2,128)S(1)}, f32[4,16,2,1024]{3,2,1,0:T(2,128)}, u32[]{:S(2)}) copy-start(f32[4,16,2,1024]{3,2,1,0:T(2,128)} %get-tuple-element.5) | copy-start | bytes 1572868
